TPU v7x, 256 devices: a whole 4x4x8 slice. The times are simulated.
256 devices in a mesh: pp: 2 (over x_hi), dp: 8 (over y, core), cp: 16 (over z, x_lo).
Axes of the slice: x: 4 (x_hi: 2, x_lo: 2; x = x_hi * 2 + x_lo), y: 4, z: 8, core: 2. Of those that a mesh axis runs over, the one named last changes fastest.
Arguments:
- tokens: bfloat16 [2, 2048, 3584], P('pp', 'cp'), may hold values from -6 to 6
- out_grad: bfloat16 [2, 2048, 3584], P('pp', 'cp'), may hold values from -6 to 6
- probs: bfloat16 [2, 2048, 8], P('pp', 'cp'), may hold values from 0.019897461 to 0.29882812
- expert_ids: int32 [2, 2048, 8], P('pp', 'cp'), may hold values from 0 to 15, all different within a row; in each aligned block of 128 rows (0 to 127, 128 to 255, ..., all dimensions but the last counted through in order) at most 80 rows name the same one
- w_gate: bfloat16 [2, 16, 1280, 3584], P('pp', 'cp', 'dp'), may hold values from -0.09375 to 0.09375
- w_up: bfloat16 [2, 16, 1280, 3584], P('pp', 'cp', 'dp'), may hold values from -0.09375 to 0.09375
- w_down: bfloat16 [2, 16, 1280, 3584], P('pp', 'cp', 'dp'), may hold values from -0.15625 to 0.15625
Outputs:
- passed_grad: bfloat16 [2, 2048, 3584], P('pp', 'cp', 'dp')
- prob_grad: float32 [2, 2048, 8], P('pp', 'cp')
- gate_grad: bfloat16 [2, 16, 1280, 3584], P('pp', 'cp', 'dp')
- up_grad: bfloat16 [2, 16, 1280, 3584], P('pp', 'cp', 'dp')
- down_grad: bfloat16 [2, 16, 1280, 3584], P('pp', 'cp', 'dp')
Inputs may be any that keep to these rules, and one draw needn't show every extreme that they name: `expert_ids`: in each aligned block of 128 tokens of a section, a token names 8 different experts, and no expert is named by more than 80 tokens of the block; some expert is named by exactly 80 tokens of some block.
All inputs are finite; a program needn't handle non-finite values.
Results may differ from a plain program's by a relative error of at most 0.012.
Values may be sent and summed in bfloat16 or wider, within the bound.
A program may use at most 128 MiB of HBM per device.

v0:
```python
import jax
import jax.numpy as jnp
from jax import lax
from jax.sharding import PartitionSpec as P

CAP_NUM, CAP_DEN = (5, 4)


def body(tokens, out_grad, probs, expert_ids, w_gate, w_up, w_down):
    tok_rows = tokens.shape[1]
    width = tokens.shape[2]
    top_count = probs.shape[2]
    experts = lax.axis_size("cp")
    replicas = lax.axis_size("dp")
    capacity = tok_rows * top_count * CAP_NUM // (CAP_DEN * experts)
    columns = width // replicas
    dp = lax.axis_index("dp")
    me = lax.axis_index("cp")
    own = lax.dynamic_slice_in_dim(jnp.stack([tokens[0], out_grad[0]]), dp * columns, columns, 2)
    blocks = lax.all_gather(own, "cp")
    ids_all = lax.all_gather(expert_ids[0], "cp")
    probs_all = lax.all_gather(probs[0], "cp")
    match = ids_all == me
    has = jnp.any(match, axis=2)
    prob_tok = jnp.sum(jnp.where(match, probs_all.astype(jnp.float32), 0.0), axis=2)
    has_i = has.astype(jnp.int32)
    slot = jnp.cumsum(has_i, axis=1) - has_i
    pick = (slot[:, None, :] == jnp.arange(capacity)[None, :, None]) & has[:, None, :]
    probs_in = jnp.sum(jnp.where(pick, prob_tok[:, None, :], 0.0), axis=2).reshape(-1, 1)
    rows = jnp.einsum(
        "bct,bstd->sbcd", pick.astype(jnp.bfloat16), blocks, preferred_element_type=jnp.float32
    ).astype(jnp.bfloat16)
    total_rows = experts * capacity
    rows = rows.reshape(2 * total_rows, columns)
    full = lax.all_gather(rows, "dp", axis=1, tiled=True)
    rows_in, grads_in = (full[:total_rows], full[total_rows:])
    gate_mat = w_gate[0, 0]
    up_mat = w_up[0, 0]
    down_mat = w_down[0, 0]
    by_feature = (((1,), (1,)), ((), ()))
    by_row = (((0,), (0,)), ((), ()))
    gate_pre = lax.dot_general(rows_in, gate_mat, by_feature, preferred_element_type=jnp.float32)
    up_pre = lax.dot_general(rows_in, up_mat, by_feature, preferred_element_type=jnp.float32)
    grad_proj = lax.dot_general(grads_in, down_mat, by_feature, preferred_element_type=jnp.float32)
    sigma = jax.nn.sigmoid(gate_pre)
    silu_gate = gate_pre * sigma
    hidden = (silu_gate * up_pre).astype(jnp.bfloat16)
    prob_part = jnp.sum(hidden.astype(jnp.float32) * grad_proj, axis=1)
    grad_hidden = probs_in * grad_proj
    grad_gate_pre = (grad_hidden * up_pre * sigma * (1.0 + gate_pre * (1.0 - sigma))).astype(
        jnp.bfloat16
    )
    grad_up_pre = (grad_hidden * silu_gate).astype(jnp.bfloat16)
    scaled_hidden = hidden
    scaled_grad = (probs_in * grads_in).astype(jnp.bfloat16)
    input_part = jnp.dot(grad_gate_pre, gate_mat, preferred_element_type=jnp.float32)
    input_part = (
        input_part + jnp.dot(grad_up_pre, up_mat, preferred_element_type=jnp.float32)
    ).astype(jnp.bfloat16)
    gate_grad = lax.dot_general(
        grad_gate_pre, rows_in, by_row, preferred_element_type=jnp.float32
    ).astype(jnp.bfloat16)
    up_grad = lax.dot_general(
        grad_up_pre, rows_in, by_row, preferred_element_type=jnp.float32
    ).astype(jnp.bfloat16)
    down_grad = lax.dot_general(
        scaled_hidden, scaled_grad, by_row, preferred_element_type=jnp.float32
    ).astype(jnp.bfloat16)
    reduced = lax.psum_scatter(input_part, "dp", scatter_dimension=1, tiled=True)
    back = lax.all_to_all(
        reduced.reshape(experts, capacity, columns), "cp", split_axis=0, concat_axis=0, tiled=True
    )
    back_probs = lax.all_to_all(
        prob_part.reshape(experts, capacity), "cp", split_axis=0, concat_axis=0, tiled=True
    )
    back_probs = lax.psum(back_probs, "dp")
    one_hot = expert_ids[0][:, :, None] == jnp.arange(experts)[None, None, :]
    has_e = jnp.any(one_hot, axis=1).astype(jnp.int32)
    slot_e = jnp.cumsum(has_e, axis=0) - has_e
    pick_e = (slot_e[:, :, None] == jnp.arange(capacity)[None, None, :]) & (has_e[:, :, None] > 0)
    input_sum = jnp.dot(
        pick_e.reshape(tok_rows, total_rows).astype(jnp.bfloat16),
        back.reshape(total_rows, columns),
        preferred_element_type=jnp.float32,
    )
    prob_te = jnp.sum(jnp.where(pick_e, back_probs[None], 0.0), axis=2)
    prob_grad = jnp.sum(jnp.where(one_hot, prob_te[:, None, :], 0.0), axis=2)
    passed = lax.ppermute(input_sum.astype(jnp.bfloat16), "pp", [(1, 0)])
    return (
        passed[None],
        prob_grad[None],
        gate_grad[None, None],
        up_grad[None, None],
        down_grad[None, None],
    )


def solution(mesh):
    in_specs = (
        P("pp", "cp", None),
        P("pp", "cp", None),
        P("pp", "cp", None),
        P("pp", "cp", None),
        P("pp", "cp", "dp", None),
        P("pp", "cp", "dp", None),
        P("pp", "cp", "dp", None),
    )
    out_specs = (
        P("pp", "cp", "dp"),
        P("pp", "cp", None),
        P("pp", "cp", "dp", None),
        P("pp", "cp", "dp", None),
        P("pp", "cp", "dp", None),
    )
    return jax.shard_map(body, mesh=mesh, in_specs=in_specs, out_specs=out_specs, check_vma=False)
```

profile of v0, /device:TPU:2, one launch (start us, length us, event | category | flops | bytes accessed | tf_op | source)
XLA Modules:
  0.0 369.4 jit_solution(6365457031545415939)
XLA Ops:
  7.2 0.0 copy-start
  7.2 0.0 copy-start.4
  7.2 0.0 copy-start.3
  7.2 0.0 all-gather.6.cloned.1.call-start
  7.3 1.6 copy.35
  8.9 1.6 copy.36
  10.5 0.7 fusion.45
  11.2 0.0 all-gather.6.cloned.1.call-update
  11.2 0.0 all-gather.4.cloned.1.call-start
  11.2 0.0 copy-done.4
  11.3 33.8 %all_gather.16 = bf16[16,128,8]{1,2,0:T(8,128)(2,1)S(1)} all-gather(bf16[1,128,8]{1,2,0:T(8,128)(2,1)S(1)} %copy-done.4), channel_id=1, replica_groups=mesh['pp'=2,'dp'=8,'cp'=16] {'cp'}, dimensions={0}, use_global_device_ids=true | all-gather | bytes 34816 | tf_op jit(solution)/shard_map/all_gather | solution.py:22
  45.1 0.0 copy-done.3
  45.1 33.9 %all_gather.15 = s32[16,128,8]{1,2,0:T(8,128)S(1)} all-gather(s32[1,128,8]{1,2,0:T(8,128)S(1)} %copy-done.3), channel_id=1, replica_groups=mesh['pp'=2,'dp'=8,'cp'=16] {'cp'}, dimensions={0}, use_global_device_ids=true | all-gather | bytes 69632 | tf_op jit(solution)/shard_map/all_gather | solution.py:21
  79.1 0.3 reduce_window_sum.23
  79.4 25.7 %all-gather.6.cloned.1.call-done = bf16[32,128,448]{1,2,0:T(8,128)(2,1)} async-done(((bf16[2,128,448]{1,2,0:T(8,128)(2,1)}), bf16[32,128,448]{1,2,0:T(8,128)(2,1)}) %all-gather.6.cloned.1.call-update) | async-done | bytes 3670032 | tf_op jit(solution)/shard_map/all_gather | solution.py:20
  105.0 3.7 convert_bitcast_fusion
  108.7 1.7 copy.37
  110.4 0.0 copy-start.2
  110.4 4.6 %copy.38 = bf16[2560,448]{0,1:T(8,128)(2,1)} copy(bf16[2560,448]{1,0:T(8,128)(2,1)} %bitcast.46) | data formatting | bytes 4587520 | tf_op jit(solution)/shard_map/reshape | solution.py:34
  115.0 0.0 all-gather.4.cloned.1.call-update
  115.0 0.2 reduce-scatter.2.cloned.1.call-start
  115.3 0.4 select_reduce_fusion.1
  115.6 0.1 mul.45
  115.7 94.2 %all-gather.4.cloned.1.call-done = bf16[2560,3584]{0,1:T(8,128)(2,1)} async-done(((bf16[2560,448]{0,1:T(8,128)(2,1)}), bf16[2560,3584]{0,1:T(8,128)(2,1)}) %all-gather.4.cloned.1.call-update) | async-done | bytes 18350096 | tf_op jit(solution)/shard_map/all_gather | solution.py:35
  209.9 0.0 copy-done.2
  209.9 0.0 copy-start.5
  210.0 5.4 %fusion.10 = f32[1280,160]{0,1:T(8,128)S(1)} fusion(bf16[2560,3584]{0,1:T(8,128)(2,1)} %all-gather.4.cloned.1.call-done, bf16[1,1,160,3584]{3,2,1,0:T(8,128)(2,1)S(1)} %copy-done.2), kind=kOutput, calls=%fused_computation.12 | convolution fusion | flops 1468006400 | bytes 11141120 | tf_op jit(solution)/shard_map/dot_general | solution.py:43
  215.4 0.0 copy-done
  215.4 0.0 copy-start.6
  215.4 6.1 %fusion.12 = f32[1280,160]{0,1:T(8,128)S(1)} fusion(bf16[2560,3584]{0,1:T(8,128)(2,1)} %all-gather.4.cloned.1.call-done, bf16[1,1,160,3584]{3,2,1,0:T(8,128)(2,1)S(1)} %copy-done), kind=kOutput, calls=%fused_computation.14 | convolution fusion | flops 1468006400 | bytes 11141120 | tf_op jit(solution)/shard_map/dot_general | solution.py:42
  221.4 0.0 copy-done.5
  221.5 0.4 copy-done.6
  221.9 3.2 multiply_reduce_fusion
  225.1 8.9 %fusion.29 = f32[1280,3584]{0,1:T(8,128)} fusion(bf16[1280,160]{0,1:T(8,128)(2,1)S(1)} %get-tuple-element.9, bf16[1,1,160,3584]{3,2,1,0:T(8,128)(2,1)S(1)} %copy-done), kind=kOutput, calls=%fused_computation.27 | convolution fusion | flops 1468006400 | bytes 19906560 | tf_op jit(solution)/shard_map/dot_general | solution.py:56
  234.0 12.3 %fusion = bf16[1280,3584]{0,1:T(8,128)(2,1)} fusion(f32[1280,3584]{0,1:T(8,128)} %fusion.29, bf16[1280,160]{0,1:T(8,128)(2,1)S(1)} %get-tuple-element.10, bf16[1,1,160,3584]{3,2,1,0:T(8,128)(2,1)S(1)} %copy-done.2), kind=kOutput, calls=%fused_computation.2 | convolution fusion | flops 1477181440 | bytes 29081600 | tf_op jit(solution)/shard_map/dot_general | solution.py:58
  246.3 0.0 reduce-scatter.2.cloned.1.call-update
  246.4 0.1 copy.32
  246.5 0.2 reduce_window_sum.22
  246.7 0.7 all_to_all.12
  247.4 8.5 %all-to-all-start.1 = ((f32[16,1,80]{2,1,0:T(1,128)}), f32[16,1,80]{2,1,0:T(1,128)S(1)}, u32[]{:S(2)}, u32[]{:S(2)}) async-start(f32[16,1,80]{2,1,0:T(1,128)} %all_to_all.12), calls=%async_computation.2 | async-start | bytes 16384 | tf_op jit(solution)/shard_map/all_to_all | solution.py:73
  255.9 0.1 copy.34
  255.9 0.1 copy.33
  256.0 49.9 %reduce-scatter.2.cloned.1.call-done = bf16[1280,448]{0,1:T(8,128)(2,1)} async-done(((bf16[1280,3584]{0,1:T(8,128)(2,1)}), bf16[1280,448]{0,1:T(8,128)(2,1)}) %reduce-scatter.2.cloned.1.call-update) | async-done | bytes 1146896 | tf_op jit(solution)/shard_map/reduce_scatter | solution.py:69
  306.0 2.4 copy.39
  308.4 0.0 all-to-all-done.1
  308.4 8.5 %all-to-all-start = ((bf16[16,80,448]{2,1,0:T(8,128)(2,1)}), bf16[16,80,448]{2,1,0:T(8,128)(2,1)S(1)}, u32[]{:S(2)}, u32[]{:S(2)}) async-start(bf16[16,80,448]{2,1,0:T(8,128)(2,1)} %bitcast.9), calls=%async_computation.1 | async-start | bytes 2621440 | tf_op jit(solution)/shard_map/all_to_all | solution.py:70
  316.9 7.8 %fusion.25 = bf16[1,1,160,3584]{3,2,1,0:T(8,128)(2,1)} fusion(bf16[1280,160]{0,1:T(8,128)(2,1)S(1)} %get-tuple-element.9, bf16[2560,3584]{0,1:T(8,128)(2,1)} %all-gather.4.cloned.1.call-done), kind=kOutput, calls=%fused_computation.21 | convolution fusion | flops 1468579840 | bytes 10731520 | tf_op jit(solution)/shard_map/dot_general | solution.py:60
  324.7 0.0 copy-start.7
  324.7 7.8 %fusion.22 = bf16[1,1,160,3584]{3,2,1,0:T(8,128)(2,1)} fusion(bf16[1280,160]{0,1:T(8,128)(2,1)S(1)} %get-tuple-element.10, bf16[2560,3584]{0,1:T(8,128)(2,1)} %all-gather.4.cloned.1.call-done), kind=kOutput, calls=%fused_computation.20 | convolution fusion | flops 1468579840 | bytes 10731520 | tf_op jit(solution)/shard_map/dot_general | solution.py:63
  332.5 0.0 copy-done.7
  332.5 0.0 copy-start.1
  332.5 7.9 %fusion.21 = bf16[1,1,160,3584]{3,2,1,0:T(8,128)(2,1)} fusion(bf16[1280,160]{0,1:T(8,128)(2,1)S(1)} %copy-done.7, f32[1280]{0:T(1024)S(1)} %mul.45, bf16[2560,3584]{0,1:T(8,128)(2,1)} %all-gather.4.cloned.1.call-done), kind=kOutput, calls=%fused_computation.19 | convolution fusion | flops 1482342400 | bytes 10736640 | tf_op jit(solution)/shard_map/dot_general | solution.py:66
  340.4 12.9 %psum.7 = f32[16,80]{1,0:T(8,128)S(1)} all-reduce(f32[16,80]{1,0:T(8,128)S(1)} %bitcast.51), channel_id=1, replica_groups=mesh['pp'=2,'dp'=8,'cp'=16] {'dp'}, use_global_device_ids=true, to_apply=%region_8.9 | all-reduce | flops 1280 | bytes 10240 | tf_op jit(solution)/shard_map/psum | solution.py:76
  353.4 0.0 all-to-all-done
  353.4 0.6 fusion.28
  354.0 1.3 collective-permute-start
  355.3 0.3 select_reduce_fusion
  355.6 0.6 select_reduce_fusion.2
  356.2 6.0 %collective-permute-done = bf16[128,448]{0,1:T(8,128)(2,1)S(1)} collective-permute-done((bf16[128,448]{0,1:T(8,128)(2,1)S(1)}, bf16[128,448]{0,1:T(8,128)(2,1)S(1)}, u32[]{:S(2)}, u32[]{:S(2)}) %collective-permute-start) | collective-permute-done | bytes 114720 | tf_op jit(solution)/shard_map/ppermute | solution.py:88
  362.2 0.6 copy.42
  362.9 0.0 copy-done.1
  (7 shorter events, 0.1 us)
Async XLA Ops:
  7.2 208.2 %copy-start = (bf16[1,1,160,3584]{3,2,1,0:T(8,128)(2,1)S(1)}, bf16[1,1,160,3584]{3,2,1,0:T(8,128)(2,1)}, u32[]{:S(2)}) copy-start(bf16[1,1,160,3584]{3,2,1,0:T(8,128)(2,1)} %param.11) | copy-start | bytes 3440644
  7.2 4.1 %copy-start.4 = (bf16[1,128,8]{1,2,0:T(8,128)(2,1)S(1)}, bf16[1,128,8]{1,2,0:T(8,128)(2,1)}, u32[]{:S(2)}) copy-start(bf16[1,128,8]{1,2,0:T(8,128)(2,1)} %param.9) | copy-start | bytes 6148
  7.2 37.9 %copy-start.3 = (s32[1,128,8]{1,2,0:T(8,128)S(1)}, s32[1,128,8]{1,2,0:T(8,128)}, u32[]{:S(2)}) copy-start(s32[1,128,8]{1,2,0:T(8,128)} %param.10) | copy-start | bytes 12292
  7.2 97.8 %all-gather.6.cloned.1.call-start = ((), (), s32[]{:S(2)}) async-start(), calls=%async_computation.5 | async-start | bytes 3899392 | tf_op jit(solution)/shard_map/all_gather | solution.py:20
  11.2 198.8 %all-gather.4.cloned.1.call-start = ((), (), s32[]{:S(2)}) async-start(), calls=%async_computation.3 | async-start | bytes 20643840 | tf_op jit(solution)/shard_map/all_gather | solution.py:35
  110.4 99.5 %copy-start.2 = (bf16[1,1,160,3584]{3,2,1,0:T(8,128)(2,1)S(1)}, bf16[1,1,160,3584]{3,2,1,0:T(8,128)(2,1)}, u32[]{:S(2)}) copy-start(bf16[1,1,160,3584]{3,2,1,0:T(8,128)(2,1)} %param.12) | copy-start | bytes 3440644
  115.0 190.9 %reduce-scatter.2.cloned.1.call-start = ((), (), s32[]{:S(2)}) async-start(), calls=%async_computation.4 | async-start | bytes 10321920 | tf_op jit(solution)/shard_map/reduce_scatter | solution.py:69
  209.9 11.5 %copy-start.5 = (bf16[2560,3584]{0,1:T(8,128)(2,1)S(1)}, bf16[2560,3584]{0,1:T(8,128)(2,1)}, u32[]{:S(2)}) copy-start(bf16[2560,3584]{0,1:T(8,128)(2,1)} %all-gather.4.cloned.1.call-done) | copy-start | bytes 55050244
  215.4 6.5 %copy-start.6 = (bf16[1,1,160,3584]{3,2,1,0:T(8,128)(2,1)S(1)}, bf16[1,1,160,3584]{3,2,1,0:T(8,128)(2,1)}, u32[]{:S(2)}) copy-start(bf16[1,1,160,3584]{3,2,1,0:T(8,128)(2,1)} %param.13) | copy-start | bytes 3440644
  247.4 61.0 %all-to-all-start.1 = ((f32[16,1,80]{2,1,0:T(1,128)}), f32[16,1,80]{2,1,0:T(1,128)S(1)}, u32[]{:S(2)}, u32[]{:S(2)}) async-start(f32[16,1,80]{2,1,0:T(1,128)} %all_to_all.12), calls=%async_computation.2 | async-start | bytes 16384 | tf_op jit(solution)/shard_map/all_to_all | solution.py:73
  308.4 45.0 %all-to-all-start = ((bf16[16,80,448]{2,1,0:T(8,128)(2,1)}), bf16[16,80,448]{2,1,0:T(8,128)(2,1)S(1)}, u32[]{:S(2)}, u32[]{:S(2)}) async-start(bf16[16,80,448]{2,1,0:T(8,128)(2,1)} %bitcast.9), calls=%async_computation.1 | async-start | bytes 2621440 | tf_op jit(solution)/shard_map/all_to_all | solution.py:70
  324.7 7.8 %copy-start.7 = (bf16[1280,160]{0,1:T(8,128)(2,1)S(1)}, bf16[1280,160]{0,1:T(8,128)(2,1)}, u32[]{:S(2)}) copy-start(bf16[1280,160]{0,1:T(8,128)(2,1)} %get-tuple-element.6) | copy-start | bytes 1228804
  332.5 30.3 %copy-start.1 = (bf16[1,1,160,3584]{3,2,1,0:T(8,128)(2,1)S(1)}, bf16[1,1,160,3584]{3,2,1,0:T(8,128)(2,1)}, u32[]{:S(2)}) copy-start(bf16[1,1,160,3584]{3,2,1,0:T(8,128)(2,1)} %param.11) | copy-start | bytes 3440644
  354.0 8.2 %collective-permute-start = (bf16[128,448]{0,1:T(8,128)(2,1)S(1)}, bf16[128,448]{0,1:T(8,128)(2,1)S(1)}, u32[]{:S(2)}, u32[]{:S(2)}) collective-permute-start(bf16[128,448]{0,1:T(8,128)(2,1)S(1)} %fusion.28), channel_id=1, source_target_pairs={{128,0},{129,1},{130,2},{131,3},{132,4},{133,5},{134,6},{135,7},{1... | collective-permute-start | bytes 344072 | tf_op jit(solution)/shard_map/ppermute | solution.py:88
Sparse Core Ops, SparseCore 0:
  11.3 93.6 all-gather.5
  115.1 94.7 all-gather.3
  246.5 59.4 reduce-scatter.1
where the time goes:
time: 370 us; the launch traced here: 369 us
  waiting for transfers between devices  176 us (48%)
  blocking collectives  80.7 us (22%)
  matrix products  63.8 us (17%)
  starting transfers between devices  18.6 us (5%)
  local copies, waits for them, and re-layouts  14 us (4%)
  between operations  13.9 us (4%)
    all_gather x1, waiting for transfers between devices, body(): full = lax.all_gather(rows, 'dp', axis=1, tiled=True)  94.2 us
    reduce_scatter x1, waiting for transfers between devices, body(): lax.psum_scatter(input_part, 'dp', scatter_dimension=1, tiled=True)  49.9 us
    all_gather x1, blocking collectives, body(): ids_all = lax.all_gather(expert_ids[0], 'cp')  33.9 us
    all_gather x1, blocking collectives, body(): probs_all = lax.all_gather(probs[0], 'cp')  33.8 us
    all_gather x1, waiting for transfers between devices, body(): blocks = lax.all_gather(own, 'cp')  25.7 us
    psum x1, blocking collectives, body(): back_probs = lax.psum(back_probs, 'dp')  12.9 us
    dot_general x1, matrix products, body(): jnp.dot(grad_up_pre, up_mat, preferred_element_type=jnp.float32)  12.3 us
    dot_general x1, matrix products, body(): jnp.dot(grad_gate_pre, gate_mat, preferred_element_type=jnp.float32)  8.93 us
  transfers between devices with their start and end apart: 6, of which 4 were waited for; matrix products, arithmetic and copies ran while one was open for 8% of the time, Pallas kernels for 0%

commit v1 on v0

--- a/solution.py
+++ b/solution.py
@@ -2,8 +2,17 @@
 import jax.numpy as jnp
 from jax import lax
 from jax.sharding import PartitionSpec as P
+from jax.lax import axis_index, axis_size, ppermute
 
 CAP_NUM, CAP_DEN = (5, 4)
+
+
+def finish_the_sectors(sample, join_dim):
+    sample = jnp.moveaxis(sample, 0, join_dim)
+    moved = sample.shape
+    return sample.reshape(
+        *moved[:join_dim], moved[join_dim] * moved[join_dim + 1], *moved[join_dim + 2 :]
+    )
 
 
 def body(tokens, out_grad, probs, expert_ids, w_gate, w_up, w_down):
@@ -32,7 +41,23 @@
     ).astype(jnp.bfloat16)
     total_rows = experts * capacity
     rows = rows.reshape(2 * total_rows, columns)
-    full = lax.all_gather(rows, "dp", axis=1, tiled=True)
+    nodes = axis_size("dp")
+    series = [(no, (no + 1) % nodes) for no in range(nodes)]
+    by_rank = [(kk, m) for m, kk in series]
+    new, part_now = ([], [])
+    it = 0
+    while it < nodes - 1:
+        if it % 2 == 0:
+            new.append(ppermute(new[-1] if new else rows, "dp", series))
+        else:
+            part_now.append(ppermute(part_now[-1] if part_now else rows, "dp", by_rank))
+        it += 1
+    e_next = jnp.stack([*new[::-1], rows, *part_now], axis=0)
+    current_block = axis_index("dp")
+    w2 = len(new)
+    mat_out = current_block - w2
+    e_next = e_next[(jnp.arange(nodes) - mat_out) % nodes]
+    full = finish_the_sectors(e_next, 1)
     rows_in, grads_in = (full[:total_rows], full[total_rows:])
     gate_mat = w_gate[0, 0]
     up_mat = w_up[0, 0]

time: 370 us -> 478 us (1.29)
  local copies, waits for them, and re-layouts: 14 us -> 114 us
  other arithmetic: 2.56 us -> 17.4 us
  waiting for transfers between devices: 176 us -> 162 us
  starting transfers between devices: 18.6 us -> 23.9 us
    all_gather x1 -> x0, waiting for transfers between devices: 94.2 us -> none  [body(): full = lax.all_gather(rows, 'dp', axis=1, tiled=True)]
    ppermute x0 -> x7, waiting for transfers between devices: none -> 81.8 us  [the longest x4 81.8 us: body(): new.append(ppermute(new[-1] if new else rows, 'dp', series))]
    slice x0 -> x3, local copies, waits for them, and re-layouts: none -> 35.7 us  [body(): rows_in, grads_in = (full[:total_rows], full[total_rows:])]
    ppermute x0 -> x7, local copies, waits for them, and re-layouts: none -> 28.8 us  [the longest x4 15.8 us: body(): new.append(ppermute(new[-1] if new else rows, 'dp', series))]
    gather x0 -> x3, local copies, waits for them, and re-layouts: none -> 26.4 us  [body(): e_next = e_next[(jnp.arange(nodes) - mat_out) % nodes]]
    transpose x0 -> x1, other arithmetic: none -> 14.8 us  [finish_the_sectors(): sample = jnp.moveaxis(sample, 0, join_dim)]
    unnamed x19 -> x46, local copies, waits for them, and re-layouts: 4.3 us -> 13.5 us
    ppermute x0 -> x7, starting transfers between devices: none -> 7.54 us  [the longest x3 7.53 us: body(): part_now.append(ppermute(part_now[-1] if part_now else rows, 'dp', by_rank))]
  transfers between devices with their start and end apart: 6 -> 12, of which waited for: 4 -> 7; matrix products, arithmetic and copies ran while one was open for 8% -> 10% of each run, Pallas kernels for 0% -> 0%
where the time goes in v1:
time: 478 us; the launch traced here: 476 us
  waiting for transfers between devices  162 us (34%)
  local copies, waits for them, and re-layouts  114 us (24%)
  blocking collectives  81.6 us (17%)
  matrix products  62.6 us (13%)
  starting transfers between devices  23.9 us (5%)
  other arithmetic  17.4 us (4%)
  between operations  14.4 us (3%)
    ppermute x4, waiting for transfers between devices, body(): new.append(ppermute(new[-1] if new else rows, 'dp', series))  81.8 us
    reduce_scatter x1, waiting for transfers between devices, body(): lax.psum_scatter(input_part, 'dp', scatter_dimension=1, tiled=True)  49.1 us
    slice x3, local copies, waits for them, and re-layouts, body(): rows_in, grads_in = (full[:total_rows], full[total_rows:])  35.7 us
    all_gather x1, blocking collectives, body(): ids_all = lax.all_gather(expert_ids[0], 'cp')  34.3 us
    all_gather x1, blocking collectives, body(): probs_all = lax.all_gather(probs[0], 'cp')  33.9 us
    gather x3, local copies, waits for them, and re-layouts, body(): e_next = e_next[(jnp.arange(nodes) - mat_out) % nodes]  26.4 us
    all_gather x1, waiting for transfers between devices, body(): blocks = lax.all_gather(own, 'cp')  25.5 us
    ppermute x4, local copies, waits for them, and re-layouts, body(): new.append(ppermute(new[-1] if new else rows, 'dp', series))  15.8 us
  transfers between devices with their start and end apart: 12, of which 7 were waited for; matrix products, arithmetic and copies ran while one was open for 10% of the time, Pallas kernels for 0%

profile of v1, /device:TPU:2, one launch (start us, length us, event | category | flops | bytes accessed | tf_op | source)
XLA Modules:
  0.0 476.5 jit_solution(5172758969801948769)
XLA Ops:
  7.2 1.6 copy.49
  8.9 1.6 copy.50
  10.4 0.7 fusion.27
  11.2 33.9 %all_gather.13 = bf16[16,128,8]{1,2,0:T(8,128)(2,1)S(1)} all-gather(bf16[1,128,8]{1,2,0:T(8,128)(2,1)} %param.9), channel_id=1, replica_groups=mesh['pp'=2,'dp'=8,'cp'=16] {'cp'}, dimensions={0}, use_global_device_ids=true | all-gather | bytes 34816 | tf_op jit(solution)/shard_map/all_gather | solution.py:31
  45.1 34.3 %all_gather.12 = s32[16,128,8]{1,2,0:T(8,128)S(1)} all-gather(s32[1,128,8]{1,2,0:T(8,128)} %param.10), channel_id=1, replica_groups=mesh['pp'=2,'dp'=8,'cp'=16] {'cp'}, dimensions={0}, use_global_device_ids=true | all-gather | bytes 69632 | tf_op jit(solution)/shard_map/all_gather | solution.py:30
  79.5 0.3 reduce_window_sum.23
  79.8 25.5 %all-gather.3.cloned.1.call-done = bf16[32,128,448]{1,2,0:T(8,128)(2,1)} async-done(((bf16[2,128,448]{1,2,0:T(8,128)(2,1)}), bf16[32,128,448]{1,2,0:T(8,128)(2,1)}) %all-gather.3.cloned.1.call-update) | async-done | bytes 3670032 | tf_op jit(solution)/shard_map/all_gather | solution.py:29
  105.3 3.7 convert_bitcast_fusion
  108.9 1.7 copy.51
  110.7 4.5 copy.52
  115.1 3.0 collective-permute-start.4
  118.1 26.0 %collective-permute-done = bf16[2560,448]{0,1:T(8,128)(2,1)S(1)} collective-permute-done((bf16[2560,448]{0,1:T(8,128)(2,1)}, bf16[2560,448]{0,1:T(8,128)(2,1)S(1)}, u32[]{:S(2)}, u32[]{:S(2)}) %collective-permute-start) | collective-permute-done | bytes 2293792 | tf_op jit(solution)/shard_map/ppermute | solution.py:51
  144.1 3.0 collective-permute-start.5
  147.1 25.8 %collective-permute-done.1 = bf16[2560,448]{0,1:T(8,128)(2,1)S(1)} collective-permute-done((bf16[2560,448]{0,1:T(8,128)(2,1)S(1)}, bf16[2560,448]{0,1:T(8,128)(2,1)S(1)}, u32[]{:S(2)}, u32[]{:S(2)}) %collective-permute-start.1) | collective-permute-done | bytes 2293792 | tf_op jit(solution)/shard_map/ppermute | solution.py:51
  172.9 1.4 copy-done.9
  174.3 1.6 collective-permute-start.6
  175.9 25.8 %collective-permute-done.2 = bf16[2560,448]{0,1:T(8,128)(2,1)} collective-permute-done((bf16[2560,448]{0,1:T(8,128)(2,1)S(1)}, bf16[2560,448]{0,1:T(8,128)(2,1)}, u32[]{:S(2)}, u32[]{:S(2)}) %collective-permute-start.2) | collective-permute-done | bytes 2293792 | tf_op jit(solution)/shard_map/ppermute | solution.py:51
  201.8 0.4 select_reduce_fusion.1
  202.2 2.6 copy.56
  204.9 4.3 copy.59
  209.2 4.3 copy.55
  213.6 4.4 copy.60
  217.9 4.4 copy.54
  222.3 4.4 copy.61
  226.7 4.2 collective-permute-done.3
  230.9 4.4 copy.53
  235.3 2.1 bitcast_dynamic-update-slice_fusion.6
  237.3 2.2 bitcast_dynamic-update-slice_fusion.5
  239.6 0.2 bitcast_dynamic-update-slice_fusion.4
  239.8 0.2 bitcast_dynamic-update-slice_fusion.3
  239.9 0.4 copy-done.1
  240.4 0.2 constant_dynamic-update-slice_fusion
  240.6 0.9 copy-done.2
  241.7 0.6 copy-done.3
  242.4 0.6 copy-done.5
  243.2 7.3 %fusion.32 = (bf16[8,1280,448]{2,1,0:T(8,128)(2,1)}, bf16[8,1280,448]{2,1,0:T(8,128)(2,1)}) fusion(bf16[8,2560,448]{2,1,0:T(8,128)(2,1)S(1)} %bitcast_dynamic-update-slice_fusion), kind=kLoop, calls=%fused_computation.70 | loop fusion | bytes 36700160 | tf_op jit(solution)/shard_map/gather | solution.py:59
  250.5 9.5 %gather_fusion = bf16[8,1280,448]{2,1,0:T(8,128)(2,1)} fusion(bf16[8,1280,448]{2,1,0:T(8,128)(2,1)} %get-tuple-element.11, s32[1024]{0:T(1024)S(1)} %pad_clamp_fusion), kind=kCustom, calls=%fused_computation | custom fusion | bytes 18350112 | tf_op jit(solution)/shard_map/gather | solution.py:59
  260.0 9.6 %gather_fusion.1 = bf16[8,1280,448]{2,1,0:T(8,128)(2,1)} fusion(bf16[8,1280,448]{2,1,0:T(8,128)(2,1)} %get-tuple-element.12, s32[1024]{0:T(1024)S(1)} %pad_clamp_fusion), kind=kCustom, calls=%fused_computation.1 | custom fusion | bytes 18350112 | tf_op jit(solution)/shard_map/gather | solution.py:59
  269.6 14.8 %maximum_bitcast_fusion = bf16[2560,8,448]{2,0,1:T(8,128)(2,1)S(1)} fusion(bf16[8,1280,448]{2,1,0:T(8,128)(2,1)} %gather_fusion.1, bf16[8,1280,448]{2,1,0:T(8,128)(2,1)} %gather_fusion), kind=kLoop, calls=%fused_computation.2 | loop fusion | flops 36700160 | bytes 36700160 | tf_op jit(solution)/shard_map/transpose | solution.py:11
  284.4 7.4 %fusion.31 = (bf16[1280,8,448]{2,0,1:T(8,128)(2,1)}, bf16[1280,8,448]{2,0,1:T(8,128)(2,1)}) fusion(bf16[2560,8,448]{2,0,1:T(8,128)(2,1)S(1)} %maximum_bitcast_fusion), kind=kLoop, calls=%fused_computation.69 | loop fusion | bytes 36700160 | tf_op jit(solution)/shard_map/slice | solution.py:61
  291.8 14.1 %copy.63 = bf16[1280,8,448]{0,2,1:T(8,128)(2,1)} copy(bf16[1280,8,448]{2,0,1:T(8,128)(2,1)} %get-tuple-element.10) | data formatting | bytes 18350080 | tf_op jit(solution)/shard_map/slice | solution.py:61
  306.0 6.3 %fusion.10 = f32[1280,160]{0,1:T(8,128)} fusion(bf16[1280,3584]{0,1:T(8,128)(2,1)} %bitcast.72, bf16[1,1,160,3584]{3,2,1,0:T(8,128)(2,1)S(1)} %copy-done), kind=kOutput, calls=%fused_computation.28 | convolution fusion | flops 1468006400 | bytes 11141120 | tf_op jit(solution)/shard_map/dot_general | solution.py:67
  312.4 0.4 slice-done.2
  312.8 2.5 fusion.13
  315.3 14.1 %copy.62 = bf16[1280,8,448]{0,2,1:T(8,128)(2,1)} copy(bf16[1280,8,448]{2,0,1:T(8,128)(2,1)} %get-tuple-element.9) | data formatting | bytes 18350080 | tf_op jit(solution)/shard_map/slice | solution.py:61
  329.5 7.0 %multiply_reduce_fusion = (f32[1280]{0:T(1024)S(1)}, bf16[1280,160]{0,1:T(8,128)(2,1)}, bf16[1280,160]{0,1:T(8,128)(2,1)S(1)}, bf16[1280,160]{0,1:T(8,128)(2,1)S(1)}) fusion(f32[1280,160]{0,1:T(8,128)} %fusion.13, f32[1280,160]{0,1:T(8,128)} %fusion.10, f32[1280]{0:T(1024)S(1)} %mul.45, bf16[1280,3584]{0,1:T(8,128)(2,1)} %bitcast.80, ...), kind=kOutput, calls=%fused_computation.35 | convolution fusion | flops 1471896320 | bytes 13199360 | tf_op jit(solution)/shard_map/dot_general | solution.py:69
  336.4 8.8 %fusion.8 = f32[1280,3584]{0,1:T(8,128)} fusion(bf16[1280,160]{0,1:T(8,128)(2,1)S(1)} %get-tuple-element.13, bf16[1,1,160,3584]{3,2,1,0:T(8,128)(2,1)S(1)} %copy-done), kind=kOutput, calls=%fused_computation.26 | convolution fusion | flops 1468006400 | bytes 19906560 | tf_op jit(solution)/shard_map/dot_general | solution.py:81
  345.3 12.5 %fusion = bf16[1280,3584]{0,1:T(8,128)(2,1)} fusion(f32[1280,3584]{0,1:T(8,128)} %fusion.8, bf16[1280,160]{0,1:T(8,128)(2,1)S(1)} %get-tuple-element.14, bf16[1,1,160,3584]{3,2,1,0:T(8,128)(2,1)S(1)} %copy-done.7), kind=kOutput, calls=%fused_computation.5 | convolution fusion | flops 1477181440 | bytes 29081600 | tf_op jit(solution)/shard_map/dot_general | solution.py:83
  357.8 0.7 all_to_all.12
  358.5 6.5 %all-to-all-start.1 = ((f32[16,1,80]{2,1,0:T(1,128)}), f32[16,1,80]{2,1,0:T(1,128)S(1)}, u32[]{:S(2)}, u32[]{:S(2)}) async-start(f32[16,1,80]{2,1,0:T(1,128)} %all_to_all.12), calls=%async_computation.2 | async-start | bytes 16384 | tf_op jit(solution)/shard_map/all_to_all | solution.py:98
  365.1 49.1 %reduce-scatter.2.cloned.1.call-done = bf16[1280,448]{0,1:T(8,128)(2,1)} async-done(((bf16[1280,3584]{0,1:T(8,128)(2,1)}), bf16[1280,448]{0,1:T(8,128)(2,1)}) %reduce-scatter.2.cloned.1.call-update) | async-done | bytes 1146896 | tf_op jit(solution)/shard_map/reduce_scatter | solution.py:94
  414.2 2.4 copy.64
  416.6 8.5 %all-to-all-start = ((bf16[16,80,448]{2,1,0:T(8,128)(2,1)}), bf16[16,80,448]{2,1,0:T(8,128)(2,1)}, u32[]{:S(2)}, u32[]{:S(2)}) async-start(bf16[16,80,448]{2,1,0:T(8,128)(2,1)} %bitcast.21), calls=%async_computation.1 | async-start | bytes 2621440 | tf_op jit(solution)/shard_map/all_to_all | solution.py:95
  425.1 0.2 reduce_window_sum.22
  425.5 7.9 %fusion.6 = bf16[1,1,160,3584]{3,2,1,0:T(8,128)(2,1)} fusion(bf16[1280,160]{0,1:T(8,128)(2,1)S(1)} %get-tuple-element.14, bf16[1280,3584]{0,1:T(8,128)(2,1)} %bitcast.73), kind=kOutput, calls=%fused_computation.13 | convolution fusion | flops 1468579840 | bytes 10731520 | tf_op jit(solution)/shard_map/dot_general | solution.py:88
  433.3 7.8 %fusion.5 = bf16[1,1,160,3584]{3,2,1,0:T(8,128)(2,1)} fusion(bf16[1280,160]{0,1:T(8,128)(2,1)S(1)} %get-tuple-element.13, bf16[1280,3584]{0,1:T(8,128)(2,1)} %bitcast.74), kind=kOutput, calls=%fused_computation.12 | convolution fusion | flops 1468579840 | bytes 10731520 | tf_op jit(solution)/shard_map/dot_general | solution.py:85
  441.2 4.2 fusion.4
  445.4 13.4 %psum.7 = f32[16,80]{1,0:T(8,128)S(1)} all-reduce(f32[16,80]{1,0:T(8,128)S(1)} %bitcast.88), channel_id=1, replica_groups=mesh['pp'=2,'dp'=8,'cp'=16] {'dp'}, use_global_device_ids=true, to_apply=%region_8.9 | all-reduce | flops 1280 | bytes 10240 | tf_op jit(solution)/shard_map/psum | solution.py:101
  458.8 1.9 fusion.7
  460.8 1.3 collective-permute-start.7
  462.1 0.3 select_reduce_fusion
  462.4 0.6 select_reduce_fusion.2
  463.0 6.0 %collective-permute-done.7 = bf16[128,448]{0,1:T(8,128)(2,1)S(1)} collective-permute-done((bf16[128,448]{0,1:T(8,128)(2,1)S(1)}, bf16[128,448]{0,1:T(8,128)(2,1)S(1)}, u32[]{:S(2)}, u32[]{:S(2)}) %collective-permute-start.7) | collective-permute-done | bytes 114720 | tf_op jit(solution)/shard_map/ppermute | solution.py:113
  469.0 0.6 copy.74
  (61 shorter events, 1.3 us)
Async XLA Ops:
  7.2 298.8 %copy-start = (bf16[1,1,160,3584]{3,2,1,0:T(8,128)(2,1)S(1)}, bf16[1,1,160,3584]{3,2,1,0:T(8,128)(2,1)}, u32[]{:S(2)}) copy-start(bf16[1,1,160,3584]{3,2,1,0:T(8,128)(2,1)} %param.11) | copy-start | bytes 3440644
  7.2 98.1 %all-gather.3.cloned.1.call-start = ((), (), s32[]{:S(2)}) async-start(), calls=%async_computation.4 | async-start | bytes 3899392 | tf_op jit(solution)/shard_map/all_gather | solution.py:29
  11.2 403.0 %reduce-scatter.2.cloned.1.call-start = ((), (), s32[]{:S(2)}) async-start(), calls=%async_computation.3 | async-start | bytes 10321920 | tf_op jit(solution)/shard_map/reduce_scatter | solution.py:94
  115.1 29.0 %collective-permute-start = (bf16[2560,448]{0,1:T(8,128)(2,1)}, bf16[2560,448]{0,1:T(8,128)(2,1)S(1)}, u32[]{:S(2)}, u32[]{:S(2)}) collective-permute-start(bf16[2560,448]{0,1:T(8,128)(2,1)} %copy.52), channel_id=1, source_target_pairs={{0,16},{16,32},{32,48},{48,64},{64,80},{80,96},{96,112},{112,0},{1... | collective-permute-start | bytes 6881288 | tf_op jit(solution)/shard_map/ppermute | solution.py:51
  115.1 29.0 %collective-permute-start.4 = (bf16[2560,448]{0,1:T(8,128)(2,1)}, bf16[2560,448]{0,1:T(8,128)(2,1)S(1)}, u32[]{:S(2)}, u32[]{:S(2)}) collective-permute-start(bf16[2560,448]{0,1:T(8,128)(2,1)} %copy.52), channel_id=1, source_target_pairs={{16,0},{32,16},{48,32},{64,48},{80,64},{96,80},{112,96},{0,112},{1... | collective-permute-start | bytes 6881288 | tf_op jit(solution)/shard_map/ppermute | solution.py:53
  144.1 28.8 %collective-permute-start.1 = (bf16[2560,448]{0,1:T(8,128)(2,1)S(1)}, bf16[2560,448]{0,1:T(8,128)(2,1)S(1)}, u32[]{:S(2)}, u32[]{:S(2)}) collective-permute-start(bf16[2560,448]{0,1:T(8,128)(2,1)S(1)} %collective-permute-done), channel_id=1, source_target_pairs={{0,16},{16,32},{32,48},{48,64},{64,80},{80,96},{96,112},{112,0},{1... | collective-permute-start | bytes 6881288 | tf_op jit(solution)/shard_map/ppermute | solution.py:51
  144.1 28.8 %copy-start.8 = (bf16[2560,448]{0,1:T(8,128)(2,1)}, bf16[2560,448]{0,1:T(8,128)(2,1)S(1)}, u32[]{:S(2)}) copy-start(bf16[2560,448]{0,1:T(8,128)(2,1)S(1)} %collective-permute-done.4) | copy-start | bytes 6881284
  144.1 28.8 %collective-permute-start.5 = (bf16[2560,448]{0,1:T(8,128)(2,1)S(1)}, bf16[2560,448]{0,1:T(8,128)(2,1)}, u32[]{:S(2)}, u32[]{:S(2)}) collective-permute-start(bf16[2560,448]{0,1:T(8,128)(2,1)S(1)} %collective-permute-done.4), channel_id=1, source_target_pairs={{16,0},{32,16},{48,32},{64,48},{80,64},{96,80},{112,96},{0,112},{1... | collective-permute-start | bytes 6881288 | tf_op jit(solution)/shard_map/ppermute | solution.py:53
  172.9 1.4 copy-start.9
  172.9 28.9 %collective-permute-start.2 = (bf16[2560,448]{0,1:T(8,128)(2,1)S(1)}, bf16[2560,448]{0,1:T(8,128)(2,1)}, u32[]{:S(2)}, u32[]{:S(2)}) collective-permute-start(bf16[2560,448]{0,1:T(8,128)(2,1)S(1)} %collective-permute-done.1), channel_id=1, source_target_pairs={{0,16},{16,32},{32,48},{48,64},{64,80},{80,96},{96,112},{112,0},{1... | collective-permute-start | bytes 6881288 | tf_op jit(solution)/shard_map/ppermute | solution.py:51
  174.3 48.0 %collective-permute-start.6 = (bf16[2560,448]{0,1:T(8,128)(2,1)}, bf16[2560,448]{0,1:T(8,128)(2,1)}, u32[]{:S(2)}, u32[]{:S(2)}) collective-permute-start(bf16[2560,448]{0,1:T(8,128)(2,1)} %collective-permute-done.5), channel_id=1, source_target_pairs={{16,0},{32,16},{48,32},{64,48},{80,64},{96,80},{112,96},{0,112},{1... | collective-permute-start | bytes 6881288 | tf_op jit(solution)/shard_map/ppermute | solution.py:53
  201.8 29.1 %collective-permute-start.3 = (bf16[2560,448]{0,1:T(8,128)(2,1)}, bf16[2560,448]{0,1:T(8,128)(2,1)}, u32[]{:S(2)}, u32[]{:S(2)}) collective-permute-start(bf16[2560,448]{0,1:T(8,128)(2,1)} %collective-permute-done.2), channel_id=1, source_target_pairs={{0,16},{16,32},{32,48},{48,64},{64,80},{80,96},{96,112},{112,0},{1... | collective-permute-start | bytes 6881288 | tf_op jit(solution)/shard_map/ppermute | solution.py:51
  235.3 4.3 copy-start.6
  235.3 4.5 copy-start.4
  237.3 3.1 copy-start.1
  239.6 1.9 copy-start.2
  239.8 2.5 copy-start.3
  239.9 3.0 copy-start.5
  306.0 6.3 %slice-start = ((s8[9175040]{0:T(1024)(128)(4,1)}), s8[4194304]{0:T(1024)(128)(4,1)S(1)}, s32[]{:S(2)}) async-start(s8[9175040]{0:T(1024)(128)(4,1)} %bitcast.75), calls=%async_computation.5 | async-start | bytes 8388608
  306.0 6.3 %copy-start.7 = (bf16[1,1,160,3584]{3,2,1,0:T(8,128)(2,1)S(1)}, bf16[1,1,160,3584]{3,2,1,0:T(8,128)(2,1)}, u32[]{:S(2)}) copy-start(bf16[1,1,160,3584]{3,2,1,0:T(8,128)(2,1)} %param.12) | copy-start | bytes 3440644
  306.0 6.4 %slice-start.1 = ((s8[9175040]{0:T(1024)(128)(4,1)}), s8[4194304]{0:T(1024)(128)(4,1)S(1)}, s32[]{:S(2)}) async-start(s8[9175040]{0:T(1024)(128)(4,1)} %bitcast.75), calls=%async_computation.6 | async-start | bytes 8388608
  306.0 6.8 %slice-start.2 = ((s8[9175040]{0:T(1024)(128)(4,1)}), s8[786432]{0:T(1024)(128)(4,1)S(1)}, s32[]{:S(2)}) async-start(s8[9175040]{0:T(1024)(128)(4,1)} %bitcast.75), calls=%async_computation.7 | async-start | bytes 1572864
  357.8 7.2 %copy-start.10 = (s32[1,128,8]{1,2,0:T(8,128)S(1)}, s32[1,128,8]{1,2,0:T(8,128)}, u32[]{:S(2)}) copy-start(s32[1,128,8]{1,2,0:T(8,128)} %param.10) | copy-start | bytes 12292
  358.5 58.1 %all-to-all-start.1 = ((f32[16,1,80]{2,1,0:T(1,128)}), f32[16,1,80]{2,1,0:T(1,128)S(1)}, u32[]{:S(2)}, u32[]{:S(2)}) async-start(f32[16,1,80]{2,1,0:T(1,128)} %all_to_all.12), calls=%async_computation.2 | async-start | bytes 16384 | tf_op jit(solution)/shard_map/all_to_all | solution.py:98
  416.6 42.2 %all-to-all-start = ((bf16[16,80,448]{2,1,0:T(8,128)(2,1)}), bf16[16,80,448]{2,1,0:T(8,128)(2,1)}, u32[]{:S(2)}, u32[]{:S(2)}) async-start(bf16[16,80,448]{2,1,0:T(8,128)(2,1)} %bitcast.21), calls=%async_computation.1 | async-start | bytes 2621440 | tf_op jit(solution)/shard_map/all_to_all | solution.py:95
  425.4 15.7 %slice-start.3 = ((s8[9175040]{0:T(1024)(128)(4,1)}), s8[4194304]{0:T(1024)(128)(4,1)S(1)}, s32[]{:S(2)}) async-start(s8[9175040]{0:T(1024)(128)(4,1)} %bitcast.81), calls=%async_computation.8 | async-start | bytes 8388608
  425.4 15.7 %slice-start.4 = ((s8[9175040]{0:T(1024)(128)(4,1)}), s8[4194304]{0:T(1024)(128)(4,1)S(1)}, s32[]{:S(2)}) async-start(s8[9175040]{0:T(1024)(128)(4,1)} %bitcast.81), calls=%async_computation.9 | async-start | bytes 8388608
  425.4 15.7 %copy-start.11 = (bf16[1280,160]{0,1:T(8,128)(2,1)S(1)}, bf16[1280,160]{0,1:T(8,128)(2,1)}, u32[]{:S(2)}) copy-start(bf16[1280,160]{0,1:T(8,128)(2,1)} %get-tuple-element.6) | copy-start | bytes 1228804
  433.3 7.8 %slice-start.5 = ((s8[9175040]{0:T(1024)(128)(4,1)}), s8[786432]{0:T(1024)(128)(4,1)S(1)}, s32[]{:S(2)}) async-start(s8[9175040]{0:T(1024)(128)(4,1)} %bitcast.81), calls=%async_computation.10 | async-start | bytes 1572864
  460.8 8.2 %collective-permute-start.7 = (bf16[128,448]{0,1:T(8,128)(2,1)S(1)}, bf16[128,448]{0,1:T(8,128)(2,1)S(1)}, u32[]{:S(2)}, u32[]{:S(2)}) collective-permute-start(bf16[128,448]{0,1:T(8,128)(2,1)S(1)} %fusion.7), channel_id=1, source_target_pairs={{128,0},{129,1},{130,2},{131,3},{132,4},{133,5},{134,6},{135,7},{1... | collective-permute-start | bytes 344072 | tf_op jit(solution)/shard_map/ppermute | solution.py:113
Sparse Core Ops, SparseCore 0:
  11.3 93.9 all-gather.2
  357.9 56.2 reduce-scatter.1
